TPU v7x, 32 devices: a whole 2x2x4 slice. The times are simulated.
32 devices in a mesh: dp: 8 (over y, x, core), mp: 4 (over z).
Axes of the slice: x: 2, y: 2, z: 4, core: 2. Of those that a mesh axis runs over, the one named last changes fastest.
Arguments:
- tokens: bfloat16 [16, 1024, 768], P('dp'), may hold values from -6 to 6
- lengths: int32 [16], P('dp'), may hold values from 256 to 1024, as said below
- qkv_weight: bfloat16 [3, 768, 768], P(None, None, 'mp'), may hold values from -0.5 to 0.5
- out_weight: bfloat16 [768, 768], P('mp'), may hold values from -0.3125 to 0.3125
- conv_taps: float32 [12, 33], P('mp'), may hold values from -0.36 to 0.36
- norm1_gain: float32 [768], replicated, may hold values from 0.1 to 1.9
- norm1_bias: float32 [768], replicated, may hold values from -0.5 to 0.5
- norm2_gain: float32 [768], replicated, may hold values from 0.1 to 1.9
- norm2_bias: float32 [768], replicated, may hold values from -0.5 to 0.5
- up_weight: bfloat16 [768, 3072], P(None, 'mp'), may hold values from -0.21875 to 0.21875
- down_weight: bfloat16 [3072, 768], P('mp'), may hold values from -0.109375 to 0.109375
- cotangent: bfloat16 [16, 1024, 768], P('dp'), may hold values from -6 to 6
Outputs:
- output: bfloat16 [16, 1024, 768], P('dp')
- input_grad: bfloat16 [16, 1024, 768], P('dp')
- qkv_grad: float32 [3, 768, 768], P(None, None, 'mp')
- out_grad: float32 [768, 768], P('mp')
- taps_grad: float32 [12, 33], P('mp')
- norm1_gain_grad: float32 [768], replicated
- norm1_bias_grad: float32 [768], replicated
- norm2_gain_grad: float32 [768], replicated
- norm2_bias_grad: float32 [768], replicated
- up_grad: float32 [768, 3072], P(None, 'mp')
- down_grad: float32 [3072, 768], P('mp')
Inputs may be any that keep to these rules, and one draw needn't show every extreme that they name: Each entry of lengths is the document's true length, and at least one document in every draw has length exactly 1024.
All inputs are finite; a program needn't handle non-finite values.
Results may differ from a plain program's by a relative error of at most 0.024.
The roundings to bfloat16 on the way count: a program that leaves them out, or rounds other values in their place, can miss the bound.
Values may be sent and summed in bfloat16 or wider, within the bound.
A program may use at most 256 MiB of HBM per device.

v0:
```python
import jax
import jax.numpy as jnp
from jax import lax
from jax.sharding import PartitionSpec as P

HEAD_DIM = 64
LANDMARKS = 64
KSIZE = 33
NS_ITERS = 6
EPSILON = 1e-05
FULL_PRECISION = lax.Precision.HIGHEST


def layer_norm(values, gain_vec, shift_vec):
    average = jnp.mean(values, axis=-1, keepdims=True)
    centered = values - average
    variance = jnp.mean(centered * centered, axis=-1, keepdims=True)
    return centered * lax.rsqrt(variance + EPSILON) * gain_vec + shift_vec


def newton_schulz(kernel):
    identity_m = jnp.eye(kernel.shape[-1], dtype=kernel.dtype)
    total_sq = jnp.sum(kernel * kernel, axis=(1, 2), keepdims=True)
    kernel_inverse = jnp.swapaxes(kernel, 1, 2) / total_sq
    for sweep_no in range(NS_ITERS):
        product = jnp.einsum("hij,hjk->hik", kernel, kernel_inverse, precision=FULL_PRECISION)
        inner_term = 7.0 * identity_m - product
        inner_term = 15.0 * identity_m - jnp.einsum(
            "hij,hjk->hik", product, inner_term, precision=FULL_PRECISION
        )
        inner_term = 13.0 * identity_m - jnp.einsum(
            "hij,hjk->hik", product, inner_term, precision=FULL_PRECISION
        )
        kernel_inverse = 0.25 * jnp.einsum(
            "hij,hjk->hik", kernel_inverse, inner_term, precision=FULL_PRECISION
        )
    return kernel_inverse


def pinv_from(landmark_queries, landmark_keys):
    scores_scale_factor = HEAD_DIM ** (-0.5)
    second_scores = (
        jnp.einsum("ble,gle->lbg", landmark_queries, landmark_keys, precision=FULL_PRECISION)
        * scores_scale_factor
    )
    return newton_schulz(jax.nn.softmax(second_scores, axis=-1))


def depthwise(values, tap_weights):
    half_span = (KSIZE - 1) // 2
    seq_len = values.shape[0]
    padded = jnp.pad(values, ((half_span, half_span), (0, 0), (0, 0)))
    running = jnp.zeros_like(values)
    for offset in range(KSIZE):
        running = (
            running + padded[offset : offset + seq_len] * tap_weights[:, offset][None, :, None]
        )
    return running


def gelu_exact(values):
    return jax.nn.gelu(values, approximate=False)


def landmark_table(length, seq_len):
    places = jnp.arange(seq_len, dtype=jnp.int32)
    live_flag = places < length
    segment = places * LANDMARKS // length
    segment_membership = (
        (segment[None, :] == jnp.arange(LANDMARKS, dtype=jnp.int32)[:, None]) & live_flag[None, :]
    ).astype(jnp.float32)
    landmark_counts = jnp.sum(segment_membership, axis=1)
    return (segment_membership, landmark_counts, live_flag)


def masked_scores(landmark_queries, key_matrix, live_flag):
    scores_scale_factor = HEAD_DIM ** (-0.5)
    third_scores = (
        jnp.einsum("xyk,pyk->yxp", landmark_queries, key_matrix, preferred_element_type=jnp.float32)
        * scores_scale_factor
    )
    return jnp.where(live_flag[None, None, :], third_scores, -1e30)


def attend_forward(query_matrix, key_matrix, value_matrix, length, tap_weights):
    scores_scale_factor = HEAD_DIM ** (-0.5)
    seq_len = query_matrix.shape[0]
    segment_membership, landmark_counts, live_flag = landmark_table(length, seq_len)
    live_f = live_flag.astype(jnp.float32)
    membership_batch = segment_membership.astype(jnp.bfloat16)
    landmark_queries = (
        jnp.einsum(
            "ov,vaf->oaf", membership_batch, query_matrix, preferred_element_type=jnp.float32
        )
        / landmark_counts[:, None, None]
    ).astype(jnp.bfloat16)
    landmark_keys = (
        jnp.einsum("ov,vaf->oaf", membership_batch, key_matrix, preferred_element_type=jnp.float32)
        / landmark_counts[:, None, None]
    ).astype(jnp.bfloat16)
    first_scores = (
        jnp.einsum("wxe,pxe->xwp", query_matrix, landmark_keys, preferred_element_type=jnp.float32)
        * scores_scale_factor
    )
    lse_one = jax.nn.logsumexp(first_scores, axis=-1)
    first_kernel = jnp.exp(first_scores - lse_one[..., None]).astype(jnp.bfloat16)
    kernel_inverse = pinv_from(
        landmark_queries.astype(jnp.float32), landmark_keys.astype(jnp.float32)
    )
    third_scores = masked_scores(landmark_queries, key_matrix, live_flag)
    lse_three = jax.nn.logsumexp(third_scores, axis=-1)
    third_kernel = jnp.exp(third_scores - lse_three[..., None]).astype(jnp.bfloat16)
    landmark_summary = jnp.einsum(
        "olp,pon->oln", third_kernel, value_matrix, preferred_element_type=jnp.float32
    )
    mixing_matrix = jnp.einsum(
        "lcb,lbf->lcf", kernel_inverse, landmark_summary, precision=FULL_PRECISION
    ).astype(jnp.bfloat16)
    landmark_approximation = jnp.einsum(
        "wpb,wbi->pwi", first_kernel, mixing_matrix, preferred_element_type=jnp.float32
    )
    masked_v = value_matrix.astype(jnp.float32) * live_f[:, None, None]
    local_term = depthwise(masked_v, tap_weights)
    context = ((landmark_approximation + local_term) * live_f[:, None, None]).astype(jnp.bfloat16)
    return (
        context,
        (
            landmark_queries,
            landmark_keys,
            lse_one,
            lse_three,
            kernel_inverse,
            landmark_summary,
            mixing_matrix,
        ),
    )


def attend_backward(
    query_matrix, key_matrix, value_matrix, length, tap_weights, kept_state, grad_context
):
    (
        landmark_queries,
        landmark_keys,
        lse_one,
        lse_three,
        kernel_inverse,
        landmark_summary,
        mixing_matrix,
    ) = kept_state
    scores_scale_factor = HEAD_DIM ** (-0.5)
    seq_len = query_matrix.shape[0]
    segment_membership, landmark_counts, live_flag = landmark_table(length, seq_len)
    live_f = live_flag.astype(jnp.float32)
    grad_local = grad_context.astype(jnp.float32) * live_f[:, None, None]
    local_branch_gradient = grad_local.astype(jnp.bfloat16)
    masked_v = value_matrix.astype(jnp.float32) * live_f[:, None, None]
    unused, conv_pull = jax.vjp(depthwise, masked_v, tap_weights)
    grad_masked, grad_taps = conv_pull(grad_local)
    first_scores = (
        jnp.einsum("wxe,pxe->xwp", query_matrix, landmark_keys, preferred_element_type=jnp.float32)
        * scores_scale_factor
    )
    first_kernel = jnp.exp(first_scores - lse_one[..., None])
    mixing_gradient = jnp.einsum(
        "paj,ape->pje",
        first_kernel.astype(jnp.bfloat16),
        local_branch_gradient,
        preferred_element_type=jnp.float32,
    )
    grad_kernel_one = jnp.einsum(
        "upn,pyn->puy", local_branch_gradient, mixing_matrix, preferred_element_type=jnp.float32
    )
    first_scores_gradient = (
        first_kernel
        * (grad_kernel_one - jnp.sum(grad_kernel_one * first_kernel, axis=-1, keepdims=True))
    ).astype(jnp.bfloat16)
    inverse_gradient = jnp.einsum(
        "xfe,xge->xfg", mixing_gradient, landmark_summary, precision=FULL_PRECISION
    )
    summary_gradient = jnp.einsum(
        "exa,exu->eau", kernel_inverse, mixing_gradient, precision=FULL_PRECISION
    ).astype(jnp.bfloat16)
    third_scores = masked_scores(landmark_queries, key_matrix, live_flag)
    third_kernel = jnp.exp(third_scores - lse_three[..., None])
    grad_kernel_three = jnp.einsum(
        "jbq,kjq->jbk", summary_gradient, value_matrix, preferred_element_type=jnp.float32
    )
    third_scores_gradient = (
        third_kernel
        * (grad_kernel_three - jnp.sum(grad_kernel_three * third_kernel, axis=-1, keepdims=True))
    ).astype(jnp.bfloat16)
    unused_inv, pinv_pull = jax.vjp(
        pinv_from, landmark_queries.astype(jnp.float32), landmark_keys.astype(jnp.float32)
    )
    landmark_query_gradient, landmark_key_gradient = pinv_pull(inverse_gradient)
    landmark_query_gradient = (
        landmark_query_gradient
        + jnp.einsum(
            "tni,itu->ntu", third_scores_gradient, key_matrix, preferred_element_type=jnp.float32
        )
        * scores_scale_factor
    )
    landmark_key_gradient = (
        landmark_key_gradient
        + jnp.einsum(
            "nxc,xnk->cnk", first_scores_gradient, query_matrix, preferred_element_type=jnp.float32
        )
        * scores_scale_factor
    )
    spread_q = jnp.einsum(
        "bq,brw->qrw",
        segment_membership,
        landmark_query_gradient / landmark_counts[:, None, None],
        precision=FULL_PRECISION,
    )
    spread_k = jnp.einsum(
        "bq,brw->qrw",
        segment_membership,
        landmark_key_gradient / landmark_counts[:, None, None],
        precision=FULL_PRECISION,
    )
    grad_query = (
        jnp.einsum(
            "nfc,cnk->fnk", first_scores_gradient, landmark_keys, preferred_element_type=jnp.float32
        )
        * scores_scale_factor
        + spread_q
    )
    grad_key = (
        jnp.einsum(
            "zpw,pzv->wzv",
            third_scores_gradient,
            landmark_queries,
            preferred_element_type=jnp.float32,
        )
        * scores_scale_factor
        + spread_k
    )
    grad_value = (
        jnp.einsum(
            "zrb,zrc->bzc",
            third_kernel.astype(jnp.bfloat16),
            summary_gradient,
            preferred_element_type=jnp.float32,
        )
        + grad_masked * live_f[:, None, None]
    )
    return (
        grad_query.astype(jnp.bfloat16),
        grad_key.astype(jnp.bfloat16),
        grad_value.astype(jnp.bfloat16),
        grad_taps,
    )


def body(
    tokens,
    lengths,
    qkv_weight,
    out_weight,
    conv_taps,
    norm1_gain,
    norm1_bias,
    norm2_gain,
    norm2_bias,
    up_weight,
    down_weight,
    cotangent,
):
    slot_count, seq_len, model_width = tokens.shape
    row_count = slot_count * seq_len
    local_heads = conv_taps.shape[0]
    local_width = local_heads * HEAD_DIM
    flat = tokens.reshape(row_count, model_width)
    places = jnp.arange(seq_len, dtype=jnp.int32)
    live_rows = (places[None, :] < lengths[:, None]).astype(jnp.float32).reshape(row_count)
    projected = jnp.einsum(
        "rd,tdc->trc", flat, qkv_weight, preferred_element_type=jnp.float32
    ).astype(jnp.bfloat16)
    per_head = projected.reshape(3, slot_count, seq_len, local_heads, HEAD_DIM)
    attend_all = jax.vmap(attend_forward, in_axes=(0, 0, 0, 0, None))
    context, kept_state = attend_all(per_head[0], per_head[1], per_head[2], lengths, conv_taps)
    context_flat = context.reshape(row_count, local_width)
    attn_part = jnp.einsum(
        "rc,cd->rd", context_flat, out_weight, preferred_element_type=jnp.float32
    )
    attn_out = lax.psum(attn_part.astype(jnp.bfloat16), "mp").astype(jnp.float32)
    mixed = flat.astype(jnp.float32) + attn_out
    normed, ln_one_pull = jax.vjp(layer_norm, mixed, norm1_gain, norm1_bias)
    normed_b = normed.astype(jnp.bfloat16)
    hidden_pre = jnp.einsum("rd,df->rf", normed_b, up_weight, preferred_element_type=jnp.float32)
    activated, gelu_pull = jax.vjp(gelu_exact, hidden_pre)
    activated_b = activated.astype(jnp.bfloat16)
    branch_part = jnp.einsum(
        "rf,fd->rd", activated_b, down_weight, preferred_element_type=jnp.float32
    )
    branch = lax.psum(branch_part.astype(jnp.bfloat16), "mp").astype(jnp.float32)
    final_norm, ln_two_pull = jax.vjp(layer_norm, normed + branch, norm2_gain, norm2_bias)
    output = (
        (final_norm * live_rows[:, None])
        .astype(jnp.bfloat16)
        .reshape(slot_count, seq_len, model_width)
    )
    grad_out = cotangent.reshape(row_count, model_width).astype(jnp.float32) * live_rows[:, None]
    grad_resid, grad_gain_two, grad_bias_two = ln_two_pull(grad_out)
    grad_branch_b = grad_resid.astype(jnp.bfloat16)
    grad_down = jnp.einsum(
        "rf,rd->fd", activated_b, grad_branch_b, preferred_element_type=jnp.float32
    )
    grad_act = jnp.einsum(
        "rd,fd->rf", grad_branch_b, down_weight, preferred_element_type=jnp.float32
    )
    grad_pre = gelu_pull(grad_act)[0].astype(jnp.bfloat16)
    grad_up = jnp.einsum("rd,rf->df", normed_b, grad_pre, preferred_element_type=jnp.float32)
    normed_part = jnp.einsum("rf,df->rd", grad_pre, up_weight, preferred_element_type=jnp.float32)
    grad_normed = grad_resid + lax.psum(normed_part.astype(jnp.bfloat16), "mp").astype(jnp.float32)
    grad_mixed, grad_gain_one, grad_bias_one = ln_one_pull(grad_normed)
    small_grads = jnp.stack([grad_gain_one, grad_bias_one, grad_gain_two, grad_bias_two])
    grad_attn_b = grad_mixed.astype(jnp.bfloat16)
    grad_outw = jnp.einsum(
        "rc,rd->cd", context_flat, grad_attn_b, preferred_element_type=jnp.float32
    )
    grad_context = jnp.einsum(
        "rd,cd->rc", grad_attn_b, out_weight, preferred_element_type=jnp.float32
    ).astype(jnp.bfloat16)
    grad_context = grad_context.reshape(slot_count, seq_len, local_heads, HEAD_DIM)
    back_all = jax.vmap(attend_backward, in_axes=(0, 0, 0, 0, None, 0, 0))
    grad_query, grad_key, grad_value, grad_taps = back_all(
        per_head[0], per_head[1], per_head[2], lengths, conv_taps, kept_state, grad_context
    )
    grad_proj = jnp.stack([grad_query, grad_key, grad_value]).reshape(3, row_count, local_width)
    grad_qkv = jnp.einsum("rd,trc->tdc", flat, grad_proj, preferred_element_type=jnp.float32)
    input_part = jnp.einsum(
        "trc,tdc->rd", grad_proj, qkv_weight, preferred_element_type=jnp.float32
    )
    input_grad = (
        grad_mixed + lax.psum(input_part.astype(jnp.bfloat16), "mp").astype(jnp.float32)
    ).astype(jnp.bfloat16)
    input_grad = input_grad.reshape(slot_count, seq_len, model_width)
    taps_pad = jnp.pad(jnp.sum(grad_taps, axis=0), ((0, 0), (0, model_width - KSIZE)))
    shares = (
        lax.psum_scatter(grad_qkv, "dp", scatter_dimension=1, tiled=True),
        lax.psum_scatter(grad_outw, "dp", scatter_dimension=1, tiled=True),
        lax.psum_scatter(taps_pad, "dp", scatter_dimension=1, tiled=True),
        lax.psum_scatter(grad_up, "dp", scatter_dimension=0, tiled=True),
        lax.psum_scatter(grad_down, "dp", scatter_dimension=1, tiled=True),
        lax.psum_scatter(small_grads, "dp", scatter_dimension=1, tiled=True),
    )
    sync_qkv, sync_outw, sync_taps, sync_up, sync_down, sync_small = (
        lax.all_gather(shares[0].astype(jnp.bfloat16), "dp", axis=1, tiled=True).astype(
            jnp.float32
        ),
        lax.all_gather(shares[1].astype(jnp.bfloat16), "dp", axis=1, tiled=True).astype(
            jnp.float32
        ),
        lax.all_gather(shares[2].astype(jnp.bfloat16), "dp", axis=1, tiled=True).astype(
            jnp.float32
        ),
        lax.all_gather(shares[3].astype(jnp.bfloat16), "dp", axis=0, tiled=True).astype(
            jnp.float32
        ),
        lax.all_gather(shares[4].astype(jnp.bfloat16), "dp", axis=1, tiled=True).astype(
            jnp.float32
        ),
        lax.all_gather(shares[5].astype(jnp.bfloat16), "dp", axis=1, tiled=True).astype(
            jnp.float32
        ),
    )
    return (
        output,
        input_grad,
        sync_qkv,
        sync_outw,
        sync_taps[:, :KSIZE],
        sync_small[0],
        sync_small[1],
        sync_small[2],
        sync_small[3],
        sync_up,
        sync_down,
    )


def solution(mesh):
    return jax.shard_map(
        body,
        mesh=mesh,
        in_specs=(
            P("dp", None, None),
            P("dp"),
            P(None, None, "mp"),
            P("mp", None),
            P("mp", None),
            P(),
            P(),
            P(),
            P(),
            P(None, "mp"),
            P("mp", None),
            P("dp", None, None),
        ),
        out_specs=(
            P("dp", None, None),
            P("dp", None, None),
            P(None, None, "mp"),
            P("mp", None),
            P("mp", None),
            P(),
            P(),
            P(),
            P(),
            P(None, "mp"),
            P("mp", None),
        ),
        check_vma=False,
    )
```

profile of v0, /device:TPU:0, one launch (start us, length us, event | category | flops | bytes accessed | tf_op | source)
XLA Modules:
  0.0 951.2 jit_solution(3927351751233964447)
XLA Ops:
  10.0 2.5 slice_reduce_fusion.36
  16.2 4.2 fusion.10
  28.3 2.2 fusion.132
  30.5 3.1 squeeze.16
  51.4 36.9 %fusion.18 = bf16[2,1024,3,64]{1,3,2,0:T(8,128)(2,1)} fusion(f32[2,1024,3,64]{1,3,2,0:T(8,128)} %convert_multiply_fusion, bf16[2,3,64,64]{3,2,1,0:T(8,128)(2,1)} %convolution_convert_fusion.6, f32[3]{0:T(128)} %get-tuple-element.140, f32[3]{0:T(128)} %get-tuple-element.141, f32[3]{0:T(128)} %get-tuple-element.110, f32[3]{0:T(128)} %get-tuple-element.111, ...), kind=kOutput, calls=%fused_computation.63 | convolution fusion | flops 77856768 | bytes 4014476 | tf_op jit(solution)/shard_map/vmap(wpb,wbi->pwi)/dot_general | solution.py:119
  91.3 2.7 convolution_convert_fusion.2
  94.1 123.9 %all-reduce.73.cloned.1.call-done = bf16[2048,768]{1,0:T(8,128)(2,1)} async-done(((bf16[2048,768]{1,0:T(8,128)(2,1)}), bf16[2048,768]{1,0:T(8,128)(2,1)}) %all-reduce.73.cloned.1.call-update) | async-done | bytes 3145744 | tf_op jit(solution)/shard_map/psum | solution.py:288
  218.0 3.9 fusion.7
  224.8 17.7 %multiply_convert_fusion.1 = (bf16[2048,768]{1,0:T(8,128)(2,1)S(1)}, f32[2048,768]{1,0:T(8,128)}, f32[2048,768]{1,0:T(8,128)}) fusion(bf16[768,768]{1,0:T(8,128)(2,1)S(1)} %copy-done, f32[2048,768]{1,0:T(8,128)S(1)} %get-tuple-element.151, f32[768]{0:T(1024)S(1)} %copy-done.118, f32[768]{0:T(1024)S(1)} %copy-done.106, f32[2048]{0:T(1024)S(1)} %fusion.107), kind=kOutput, calls=%fused_computation.17 | convolution fusion | flops 2524446720 | bytes 23214080 | tf_op jit(solution)/shard_map/rd,df->rf/dot_general | solution.py:292
  244.3 3.9 convolution_convert_fusion.1
  248.9 119.6 %all-reduce.75.cloned.1.call-done = bf16[2048,768]{1,0:T(8,128)(2,1)} async-done(((bf16[2048,768]{1,0:T(8,128)(2,1)}), bf16[2048,768]{1,0:T(8,128)(2,1)}) %all-reduce.75.cloned.1.call-update) | async-done | bytes 3145744 | tf_op jit(solution)/shard_map/psum | solution.py:298
  368.5 4.6 fusion.126
  375.0 2.6 multiply_reduce_fusion.1
  377.7 4.9 fusion.125
  382.6 4.6 add_convert_fusion.1
  389.0 4.0 convolution_convert_fusion
  393.4 7.9 fusion.112
  401.5 2.7 multiply_reduce_fusion
  405.4 7.1 fusion.114
  412.5 100.7 %all-reduce.77.cloned.1.call-done = bf16[2048,768]{1,0:T(8,128)(2,1)} async-done(((bf16[2048,768]{1,0:T(8,128)(2,1)}), bf16[2048,768]{1,0:T(8,128)(2,1)}) %all-reduce.77.cloned.1.call-update) | async-done | bytes 3145744 | tf_op jit(solution)/shard_map/psum | solution.py:317
  513.2 7.0 multiply_reduce_fusion.2
  520.3 6.7 fusion.124
  527.0 2.6 copy-done.6
  529.6 2.5 fusion.11
  532.1 2.8 reshape.458
  562.9 7.8 multiply_reduce_fusion.39
  570.7 8.4 multiply_reduce_fusion.38
  588.4 2.6 convolution_bitcast_fusion.1
  594.9 2.4 multiply_convert_fusion.3
  599.9 8.6 broadcast_multiply_fusion.1
  611.1 9.5 %broadcast_multiply_fusion = (f32[2,1024,3,64]{1,3,2,0:T(8,128)}, f32[2,1024,3,64]{1,3,2,0:T(8,128)}, f32[2,1024,3,64]{1,3,2,0:T(8,128)}, f32[2,1024,3,64]{1,3,2...) fusion(f32[3]{0:T(128)S(1)} %copy-done.142, ...), kind=kLoop, calls=%fused_computation.230 | loop fusion | flops 7077888 | bytes 28319948 | tf_op jit(solution)/shard_map/vmap(transpose(jvp()))/mul | solution.py:56
  620.7 20.5 %pad_add_fusion = f32[2,1056,3,64]{1,3,2,0:T(8,128)} fusion(f32[2,1024,3,64]{1,3,2,0:T(8,128)} %get-tuple-element.160, f32[2,1024,3,64]{1,3,2,0:T(8,128)} %get-tuple-element.161, f32[2,1024,3,64]{1,3,2,0:T(8,128)} %get-tuple-element.162, f32[2,1024,3,64]{1,3,2,0:T(8,128)} %get-tuple-element.163, f32[2,1024,3,64]{1,3,2,0:T(8,128)} %get-tuple-element.164, ...), kind=kLoop, calls=%fused_computation.47 | loop fusion | flops 10543104 | bytes 44089344 | tf_op jit(solution)/shard_map/vmap(transpose(jvp()))/add_any | solution.py:56
  649.3 7.5 fusion.14
  662.8 2.7 copy.302
  665.5 4.8 reshape.471
  671.5 4.0 bitcast_convert_fusion
  676.4 8.8 all-gather
  686.7 8.8 all-gather.1
  696.3 21.4 %reduce-scatter.21.cloned.1.call-done = f32[96,192]{1,0:T(8,128)} async-done(((f32[768,192]{1,0:T(8,128)}), f32[96,192]{1,0:T(8,128)}) %reduce-scatter.21.cloned.1.call-update) | async-done | bytes 73744
  718.7 9.5 %all_gather.19 = bf16[192,768]{0,1:T(8,128)(2,1)S(1)} all-gather(bf16[192,96]{0,1:T(8,128)(2,1)S(1)} %copy.262), channel_id=1, replica_groups=mesh['dp'=8,'mp'=4] {'dp'}, dimensions={1}, use_global_device_ids=true | all-gather | bytes 331776 | tf_op jit(solution)/shard_map/all_gather | solution.py:354
  729.2 14.4 %all-gather.7.cloned.1.call-done = bf16[768,768]{0,1:T(8,128)(2,1)} async-done(((bf16[768,96]{0,1:T(8,128)(2,1)}), bf16[768,768]{0,1:T(8,128)(2,1)}) %all-gather.7.cloned.1.call-update) | async-done | bytes 1179664 | tf_op jit(solution)/shard_map/all_gather | solution.py:363
  743.6 2.7 copy.268
  746.3 23.7 %all-gather.5.cloned.1.call-done = bf16[768,768]{1,0:T(8,128)(2,1)} async-done(((bf16[96,768]{1,0:T(8,128)(2,1)}), bf16[768,768]{1,0:T(8,128)(2,1)}) %all-gather.5.cloned.1.call-update) | async-done | bytes 1179664 | tf_op jit(solution)/shard_map/all_gather | solution.py:360
  770.0 2.8 convert_element_type.248
  772.9 40.9 %reduce-scatter.19.cloned.1.call-done = f32[96,576]{1,0:T(8,128)} async-done(((f32[768,576]{1,0:T(8,128)}), f32[96,576]{1,0:T(8,128)}) %reduce-scatter.19.cloned.1.call-update) | async-done | bytes 221200
  815.2 12.1 %all_gather.18 = bf16[3,768,192]{2,0,1:T(4,128)(2,1)S(1)} all-gather(bf16[3,96,192]{2,0,1:T(4,128)(2,1)S(1)} %copy.261), channel_id=1, replica_groups=mesh['dp'=8,'mp'=4] {'dp'}, dimensions={1}, use_global_device_ids=true | all-gather | bytes 995328 | tf_op jit(solution)/shard_map/all_gather | solution.py:351
  829.5 108.3 %all-reduce.79.cloned.1.call-done = bf16[2048,768]{1,0:T(8,128)(2,1)} async-done(((bf16[2048,768]{1,0:T(8,128)(2,1)}), bf16[2048,768]{1,0:T(8,128)(2,1)}) %all-reduce.79.cloned.1.call-update) | async-done | bytes 3145744 | tf_op jit(solution)/shard_map/psum | solution.py:338
  937.8 6.3 add_convert_fusion
  (534 shorter events, 114.0 us)
Async XLA Ops:
  7.2 217.6 %copy-start = (bf16[768,768]{1,0:T(8,128)(2,1)S(1)}, bf16[768,768]{1,0:T(8,128)(2,1)}, u32[]{:S(2)}) copy-start(bf16[768,768]{1,0:T(8,128)(2,1)} %param.23) | copy-start | bytes 3538948
  7.2 210.8 %all-reduce.73.cloned.1.call-start = ((), (), s32[]{:S(2)}) async-start(), calls=%async_computation.6 | async-start | bytes 6291456 | tf_op jit(solution)/shard_map/psum | solution.py:288
  15.0 11.0 %copy-start.99 = (pred[2,1024]{1,0:T(4,128)(4,1)}, pred[2,1024]{1,0:T(4,128)(4,1)S(1)}, u32[]{:S(2)}) copy-start(pred[2,1024]{1,0:T(4,128)(4,1)S(1)} %get-tuple-element.191) | copy-start | bytes 6148
  23.5 4.8 copy-start.36
  26.7 3.8 copy-start.83
  27.3 18.4 %copy-start.104 = (f32[2,3,64]{2,1,0:T(4,128)}, f32[2,3,64]{2,1,0:T(4,128)S(1)}, u32[]{:S(2)}) copy-start(f32[2,3,64]{2,1,0:T(4,128)S(1)} %get-tuple-element.194) | copy-start | bytes 4612
  27.3 20.8 %copy-start.3 = (f32[2,3,64,1024]{3,2,1,0:T(8,128)}, f32[2,3,64,1024]{3,2,1,0:T(8,128)S(1)}, u32[]{:S(2)}) copy-start(f32[2,3,64,1024]{3,2,1,0:T(8,128)S(1)} %get-tuple-element.195) | copy-start | bytes 4718596
  34.7 9.3 copy-start.17
  45.7 4.7 copy-start.77
  88.2 3.1 copy-start.82
  94.1 274.4 %all-reduce.75.cloned.1.call-start = ((), (), s32[]{:S(2)}) async-start(), calls=%async_computation.7 | async-start | bytes 6291456 | tf_op jit(solution)/shard_map/psum | solution.py:298
  218.0 3.9 copy-start.14
  218.0 4.7 copy-start.16
  224.7 17.8 %copy-start.2 = (f32[2048,768]{1,0:T(8,128)}, f32[2048,768]{1,0:T(8,128)S(1)}, u32[]{:S(2)}) copy-start(f32[2048,768]{1,0:T(8,128)S(1)} %get-tuple-element.151) | copy-start | bytes 18874372
  224.8 19.5 %copy-start.155 = (bf16[768,768]{1,0:T(8,128)(2,1)S(1)}, bf16[768,768]{1,0:T(8,128)(2,1)}, u32[]{:S(2)}) copy-start(bf16[768,768]{1,0:T(8,128)(2,1)} %param.24) | copy-start | bytes 3538948
  248.2 265.0 %all-reduce.77.cloned.1.call-start = ((), (), s32[]{:S(2)}) async-start(), calls=%async_computation.8 | async-start | bytes 6291456 | tf_op jit(solution)/shard_map/psum | solution.py:317
  375.0 7.6 slice-start.2
  375.0 7.6 slice-start.4
  377.7 4.9 slice-start.3
  377.7 4.9 slice-start.5
  382.6 4.7 copy-start.7
  393.0 215.6 %reduce-scatter.17.cloned.1.call-start = ((), (), s32[]{:S(2)}) async-start(), calls=%async_computation.12 | async-start | bytes 2654208 | tf_op jit(solution)/shard_map/reduce_scatter | solution.py:347
  401.4 3.4 copy-start.114
  401.4 239.8 %reduce-scatter.15.cloned.1.call-start = ((), (), s32[]{:S(2)}) async-start(), calls=%async_computation.10 | async-start | bytes 2654208 | tf_op jit(solution)/shard_map/reduce_scatter | solution.py:346
  401.4 3.9 copy-start.161
  412.5 263.1 %reduce-scatter.23.cloned.1.call-start = ((), (), s32[]{:S(2)}) async-start(), calls=%async_computation.16 | async-start | bytes 442368
  513.2 7.0 copy-start.13
  527.0 5.1 copy-start.101
  535.0 3.2 copy-start.49
  562.9 7.8 copy-start.151
  570.7 9.3 copy-start.66
  579.2 4.9 copy-start.41
  581.5 6.9 slice-start
  583.7 4.6 slice-start.1
  591.0 94.8 %reduce-scatter.25.cloned.1.call-start = ((), (), s32[]{:S(2)}) async-start(), calls=%async_computation.17 | async-start | bytes 442368
  592.8 124.8 %reduce-scatter.21.cloned.1.call-start = ((), (), s32[]{:S(2)}) async-start(), calls=%async_computation.15 | async-start | bytes 884736
  594.8 148.8 %all-gather.7.cloned.1.call-start = ((), (), s32[]{:S(2)}) async-start(), calls=%async_computation.13 | async-start | bytes 1327104 | tf_op jit(solution)/shard_map/all_gather | solution.py:363
  599.8 10.7 %copy-start.84 = (bf16[2,64,3,64]{3,1,2,0:T(8,128)(2,1)S(1)}, bf16[2,64,3,64]{3,1,2,0:T(8,128)(2,1)}, u32[]{:S(2)}) copy-start(bf16[2,64,3,64]{3,1,2,0:T(8,128)(2,1)} %copy-done.83) | copy-start | bytes 147460
  599.8 10.7 %copy-start.116 = (f32[2,3,64]{2,1,0:T(4,128)S(1)}, f32[2,3,64]{2,1,0:T(4,128)}, u32[]{:S(2)}) copy-start(f32[2,3,64]{2,1,0:T(4,128)} %neg.102) | copy-start | bytes 4612
  599.8 10.7 %copy-start.154 = (f32[2,64]{1,0:T(2,128)S(1)}, f32[2,64]{1,0:T(2,128)}, u32[]{:S(2)}) copy-start(f32[2,64]{1,0:T(2,128)} %copy-done.152) | copy-start | bytes 1540
  599.9 10.7 %copy-start.157 = (f32[2,64,3,64]{3,1,2,0:T(8,128)S(1)}, f32[2,64,3,64]{3,1,2,0:T(8,128)}, u32[]{:S(2)}) copy-start(f32[2,64,3,64]{3,1,2,0:T(8,128)} %fusion.40) | copy-start | bytes 294916
  599.9 10.7 %copy-start.159 = (f32[2,3,64,64]{2,3,1,0:T(8,128)S(1)}, f32[2,3,64,64]{2,3,1,0:T(8,128)}, u32[]{:S(2)}) copy-start(f32[2,3,64,64]{2,3,1,0:T(8,128)} %get-tuple-element.204) | copy-start | bytes 294916
  610.3 159.7 %all-gather.5.cloned.1.call-start = ((), (), s32[]{:S(2)}) async-start(), calls=%async_computation.11 | async-start | bytes 1327104 | tf_op jit(solution)/shard_map/all_gather | solution.py:360
  642.9 170.9 %reduce-scatter.19.cloned.1.call-start = ((), (), s32[]{:S(2)}) async-start(), calls=%async_computation.14 | async-start | bytes 2211840
  665.5 5.1 copy-start.96
  670.3 267.5 %all-reduce.79.cloned.1.call-start = ((), (), s32[]{:S(2)}) async-start(), calls=%async_computation.9 | async-start | bytes 6291456 | tf_op jit(solution)/shard_map/psum | solution.py:338
  827.3 110.5 %copy-start.103 = (f32[2048]{0:T(1024)S(1)}, f32[2048]{0:T(1024)}, u32[]{:S(2)}) copy-start(f32[2048]{0:T(1024)} %copy-done.101) | copy-start | bytes 24580
  937.8 6.3 copy-start.1
  (133 other events, 244.5 us)
Sparse Core Ops, SparseCore 0:
  94.2 123.7 all-reduce.72
  248.4 120.0 all-reduce.74
  393.1 120.0 all-reduce.76
  517.0 41.5 reduce-scatter.16
  562.7 42.4 reduce-scatter.14
  608.7 33.8 reduce-scatter.22
  645.6 33.7 reduce-scatter.24
  682.6 34.9 reduce-scatter.20
  719.5 24.0 all-gather.6
  745.9 24.0 all-gather.4
  773.4 40.3 reduce-scatter.18
  816.7 121.0 all-reduce.78
where the time goes:
time: 957 us; the launch traced here: 951 us
  waiting for transfers between devices  553 us (58%)
  matrix products  160 us (17%)
  other arithmetic  116 us (12%)
  local copies, waits for them, and re-layouts  63.3 us (7%)
  blocking collectives  39.2 us (4%)
  between operations  17.5 us (2%)
    psum x1, waiting for transfers between devices, body(): lax.psum(attn_part.astype(jnp.bfloat16), 'mp').astype(jnp.float32)  124 us
    psum x1, waiting for transfers between devices, body(): lax.psum(branch_part.astype(jnp.bfloat16), 'mp').astype(jnp.float32)  120 us
    psum x1, waiting for transfers between devices, body(): lax.psum(input_part.astype(jnp.bfloat16), 'mp').astype(jnp.float32)  108 us
    psum x1, waiting for transfers between devices, body(): lax.psum(normed_part.astype(jnp.bfloat16), 'mp').astype(jnp.float32)  101 us
    unnamed x16, waiting for transfers between devices  62.5 us
    unnamed x355, local copies, waits for them, and re-layouts  39 us
    dot_general x1, matrix products, attend_forward(): jnp.einsum('wpb,wbi->pwi', first_kernel, mixing_matrix, preferred_element...  36.9 us
    all_gather x1, waiting for transfers between devices, body(): lax.all_gather(shares[3].astype(jnp.bfloat16), 'dp', axis=0, tiled=True)  23.7 us
  transfers between devices with their start and end apart: 12, of which 8 were waited for; matrix products, arithmetic and copies ran while one was open for 19% of the time, Pallas kernels for 0%

commit v1 on v0

--- a/solution.py
+++ b/solution.py
@@ -9,6 +9,7 @@
 NS_ITERS = 6
 EPSILON = 1e-05
 FULL_PRECISION = lax.Precision.HIGHEST
+_balance_groups = lambda z: lax.all_gather(z, "mp").sum(axis=0)
 
 
 def layer_norm(values, gain_vec, shift_vec):
@@ -335,7 +336,7 @@
         "trc,tdc->rd", grad_proj, qkv_weight, preferred_element_type=jnp.float32
     )
     input_grad = (
-        grad_mixed + lax.psum(input_part.astype(jnp.bfloat16), "mp").astype(jnp.float32)
+        grad_mixed + _balance_groups(input_part.astype(jnp.bfloat16)).astype(jnp.float32)
     ).astype(jnp.bfloat16)
     input_grad = input_grad.reshape(slot_count, seq_len, model_width)
     taps_pad = jnp.pad(jnp.sum(grad_taps, axis=0), ((0, 0), (0, model_width - KSIZE)))

time: 957 us -> 1060 us (1.11)
  waiting for transfers between devices: 553 us -> 627 us
  matrix products: 160 us -> 177 us
    all_gather x0 -> x1, waiting for transfers between devices: none -> 205 us  [_balance_groups = lambda z: lax.all_gather(z, 'mp').sum(axis=0)]
    psum x1 -> x0, waiting for transfers between devices: 108 us -> none  [body(): lax.psum(input_part.astype(jnp.bfloat16), 'mp').astype(jnp.float32)]
    unnamed x16, waiting for transfers between devices: 62.5 us -> 41.2 us
    unnamed x355 -> x341, local copies, waits for them, and re-layouts: 39 us -> 35.4 us
  transfers between devices with their start and end apart: 12 -> 12, of which waited for: 8 -> 7; matrix products, arithmetic and copies ran while one was open for 19% -> 20% of each run, Pallas kernels for 0% -> 0%
where the time goes in v1:
time: 1060 us
  waiting for transfers between devices  627 us (59%)
  matrix products  177 us (17%)
  other arithmetic  125 us (12%)
  local copies, waits for them, and re-layouts  70.3 us (7%)
  blocking collectives  38.7 us (4%)
  between operations  17.3 us (2%)
    all_gather x1, waiting for transfers between devices, _balance_groups = lambda z: lax.all_gather(z, 'mp').sum(axis=0)  205 us
    psum x1, waiting for transfers between devices, body(): lax.psum(attn_part.astype(jnp.bfloat16), 'mp').astype(jnp.float32)  124 us
    psum x1, waiting for transfers between devices, body(): lax.psum(branch_part.astype(jnp.bfloat16), 'mp').astype(jnp.float32)  120 us
    psum x1, waiting for transfers between devices, body(): lax.psum(normed_part.astype(jnp.bfloat16), 'mp').astype(jnp.float32)  99.8 us
    unnamed x16, waiting for transfers between devices  41.2 us
    dot_general x1, matrix products, attend_forward(): jnp.einsum('wpb,wbi->pwi', first_kernel, mixing_matrix, preferred_element...  37.5 us
    unnamed x341, local copies, waits for them, and re-layouts  35.4 us
    all_gather x1, waiting for transfers between devices, body(): lax.all_gather(shares[3].astype(jnp.bfloat16), 'dp', axis=0, tiled=True)  23.1 us
  transfers between devices with their start and end apart: 12, of which 7 were waited for; matrix products, arithmetic and copies ran while one was open for 20% of the time, Pallas kernels for 0%

profile of v1, /device:TPU:0, one launch (start us, length us, event | category | flops | bytes accessed | tf_op | source)
XLA Modules:
  0.0 1056.1 jit_solution(5863120822550070500)
XLA Ops:
  13.9 4.2 fusion.10
  28.1 3.4 squeeze.16
  49.8 37.5 %fusion.18 = bf16[2,1024,3,64]{1,3,2,0:T(8,128)(2,1)} fusion(f32[2,1024,3,64]{1,3,2,0:T(8,128)} %convert_multiply_fusion, bf16[2,3,64,64]{3,2,1,0:T(8,128)(2,1)} %convolution_convert_fusion.6, f32[3]{0:T(128)} %get-tuple-element.140, f32[3]{0:T(128)} %get-tuple-element.141, f32[3]{0:T(128)} %get-tuple-element.110, f32[3]{0:T(128)} %get-tuple-element.111, ...), kind=kOutput, calls=%fused_computation.63 | convolution fusion | flops 77856768 | bytes 4014476 | tf_op jit(solution)/shard_map/vmap(wpb,wbi->pwi)/dot_general | solution.py:120
  90.3 2.7 convolution_convert_fusion.2
  93.1 123.9 %all-reduce.72.cloned.1.call-done = bf16[2048,768]{1,0:T(8,128)(2,1)} async-done(((bf16[2048,768]{1,0:T(8,128)(2,1)}), bf16[2048,768]{1,0:T(8,128)(2,1)}) %all-reduce.72.cloned.1.call-update) | async-done | bytes 3145744 | tf_op jit(solution)/shard_map/psum | solution.py:289
  217.0 3.9 fusion.7
  223.6 17.7 %multiply_convert_fusion.1 = (bf16[2048,768]{1,0:T(8,128)(2,1)S(1)}, f32[2048,768]{1,0:T(8,128)}, f32[2048,768]{1,0:T(8,128)}) fusion(bf16[768,768]{1,0:T(8,128)(2,1)S(1)} %copy-done, f32[2048,768]{1,0:T(8,128)S(1)} %get-tuple-element.151, f32[768]{0:T(1024)S(1)} %copy-done.114, f32[768]{0:T(1024)S(1)} %copy-done.102, f32[2048]{0:T(1024)S(1)} %fusion.107), kind=kOutput, calls=%fused_computation.17 | convolution fusion | flops 2524446720 | bytes 23214080 | tf_op jit(solution)/shard_map/rd,df->rf/dot_general | solution.py:293
  243.1 3.9 convolution_convert_fusion.1
  247.7 119.6 %all-reduce.74.cloned.1.call-done = bf16[2048,768]{1,0:T(8,128)(2,1)} async-done(((bf16[2048,768]{1,0:T(8,128)(2,1)}), bf16[2048,768]{1,0:T(8,128)(2,1)}) %all-reduce.74.cloned.1.call-update) | async-done | bytes 3145744 | tf_op jit(solution)/shard_map/psum | solution.py:299
  367.3 4.8 fusion.126
  374.0 2.6 multiply_reduce_fusion.1
  376.7 4.9 fusion.125
  381.6 5.4 add_convert_fusion.1
  387.0 6.2 convolution_convert_fusion
  393.3 7.9 fusion.112
  401.5 2.7 multiply_reduce_fusion
  406.6 7.0 fusion.114
  413.7 99.8 %all-reduce.76.cloned.1.call-done = bf16[2048,768]{1,0:T(8,128)(2,1)} async-done(((bf16[2048,768]{1,0:T(8,128)(2,1)}), bf16[2048,768]{1,0:T(8,128)(2,1)}) %all-reduce.76.cloned.1.call-update) | async-done | bytes 3145744 | tf_op jit(solution)/shard_map/psum | solution.py:318
  513.5 7.6 multiply_reduce_fusion.2
  521.1 8.2 fusion.124
  530.0 5.2 fusion.11
  535.2 3.0 reshape.458
  566.3 7.8 multiply_reduce_fusion.39
  574.1 8.2 multiply_reduce_fusion.38
  591.3 5.5 convolution_bitcast_fusion.1
  602.4 2.9 fusion.56
  610.5 8.6 broadcast_multiply_fusion.1
  624.6 9.6 broadcast_multiply_fusion
  634.2 20.6 %pad_add_fusion = f32[2,1056,3,64]{1,3,2,0:T(8,128)} fusion(f32[2,1024,3,64]{1,3,2,0:T(8,128)} %get-tuple-element.160, f32[2,1024,3,64]{1,3,2,0:T(8,128)} %get-tuple-element.161, f32[2,1024,3,64]{1,3,2,0:T(8,128)} %get-tuple-element.162, f32[2,1024,3,64]{1,3,2,0:T(8,128)} %get-tuple-element.163, f32[2,1024,3,64]{1,3,2,0:T(8,128)} %get-tuple-element.164, ...), kind=kLoop, calls=%fused_computation.47 | loop fusion | flops 10543104 | bytes 44089344 | tf_op jit(solution)/shard_map/vmap(transpose(jvp()))/add_any | solution.py:57
  657.3 2.8 copy.253
  660.2 3.4 stack.19
  666.8 3.2 stack.20
  670.1 6.9 fusion.14
  683.0 2.7 copy.302
  685.7 4.6 reshape.472
  691.5 6.0 bitcast_convert_fusion
  698.5 9.0 all-gather.1
  709.0 8.8 all-gather.2
  719.6 8.9 all_gather.27
  729.5 14.4 %all-gather.9.cloned.1.call-done = bf16[768,768]{0,1:T(8,128)(2,1)} async-done(((bf16[768,96]{0,1:T(8,128)(2,1)}), bf16[768,768]{0,1:T(8,128)(2,1)}) %all-gather.9.cloned.1.call-update) | async-done | bytes 1179664 | tf_op jit(solution)/shard_map/all_gather | solution.py:364
  743.9 2.7 copy.268
  746.6 23.1 %all-gather.7.cloned.1.call-done = bf16[768,768]{1,0:T(8,128)(2,1)} async-done(((bf16[96,768]{1,0:T(8,128)(2,1)}), bf16[768,768]{1,0:T(8,128)(2,1)}) %all-gather.7.cloned.1.call-update) | async-done | bytes 1179664 | tf_op jit(solution)/shard_map/all_gather | solution.py:361
  769.7 2.8 convert_element_type.250
  772.5 40.9 %reduce-scatter.19.cloned.1.call-done = f32[96,576]{1,0:T(8,128)} async-done(((f32[768,576]{1,0:T(8,128)}), f32[96,576]{1,0:T(8,128)}) %reduce-scatter.19.cloned.1.call-update) | async-done | bytes 221200
  814.9 12.1 %all_gather.26 = bf16[3,768,192]{2,0,1:T(4,128)(2,1)S(1)} all-gather(bf16[3,96,192]{2,0,1:T(4,128)(2,1)S(1)} %copy.261), channel_id=1, replica_groups=mesh['dp'=8,'mp'=4] {'dp'}, dimensions={1}, use_global_device_ids=true | all-gather | bytes 995328 | tf_op jit(solution)/shard_map/all_gather | solution.py:352
  829.2 204.6 %all-gather.11.cloned.1.call-done = bf16[8192,768]{1,0:T(8,128)(2,1)} async-done(((bf16[2048,768]{1,0:T(8,128)(2,1)}), bf16[8192,768]{1,0:T(8,128)(2,1)}) %all-gather.11.cloned.1.call-update) | async-done | bytes 12582928 | tf_op jit(solution)/shard_map/all_gather | solution.py:12
  1033.8 9.0 reduce_sum.525
  1042.8 6.3 add_convert_fusion
  (520 shorter events, 121.3 us)
Async XLA Ops:
  7.2 216.4 %copy-start = (bf16[768,768]{1,0:T(8,128)(2,1)S(1)}, bf16[768,768]{1,0:T(8,128)(2,1)}, u32[]{:S(2)}) copy-start(bf16[768,768]{1,0:T(8,128)(2,1)} %param.23) | copy-start | bytes 3538948
  7.2 209.8 %all-reduce.72.cloned.1.call-start = ((), (), s32[]{:S(2)}) async-start(), calls=%async_computation.6 | async-start | bytes 6291456 | tf_op jit(solution)/shard_map/psum | solution.py:289
  13.9 10.1 copy-start.96
  13.9 18.9 %copy-start.76 = (f32[64,64]{1,0:T(8,128)}, f32[64,64]{1,0:T(8,128)S(1)}, u32[]{:S(2)}) copy-start(f32[64,64]{1,0:T(8,128)S(1)} %fusion.106) | copy-start | bytes 49156
  13.9 20.8 %copy-start.28 = (f32[64,64]{1,0:T(8,128)}, f32[64,64]{1,0:T(8,128)S(1)}, u32[]{:S(2)}) copy-start(f32[64,64]{1,0:T(8,128)S(1)} %get-tuple-element.209) | copy-start | bytes 49156
  13.9 20.8 %copy-start.78 = (f32[64,64]{1,0:T(8,128)}, f32[64,64]{1,0:T(8,128)S(1)}, u32[]{:S(2)}) copy-start(f32[64,64]{1,0:T(8,128)S(1)} %get-tuple-element.210) | copy-start | bytes 49156
  25.2 18.8 %copy-start.100 = (f32[2,3,64]{2,1,0:T(4,128)}, f32[2,3,64]{2,1,0:T(4,128)S(1)}, u32[]{:S(2)}) copy-start(f32[2,3,64]{2,1,0:T(4,128)S(1)} %get-tuple-element.194) | copy-start | bytes 4612
  47.1 40.2 %copy-start.71 = (f32[2,3,64,64]{3,2,1,0:T(8,128)}, f32[2,3,64,64]{3,2,1,0:T(8,128)S(1)}, u32[]{:S(2)}) copy-start(f32[2,3,64,64]{3,2,1,0:T(8,128)S(1)} %fusion.45) | copy-start | bytes 294916
  93.1 274.2 %all-reduce.74.cloned.1.call-start = ((), (), s32[]{:S(2)}) async-start(), calls=%async_computation.7 | async-start | bytes 6291456 | tf_op jit(solution)/shard_map/psum | solution.py:299
  223.6 17.8 %copy-start.2 = (f32[2048,768]{1,0:T(8,128)}, f32[2048,768]{1,0:T(8,128)S(1)}, u32[]{:S(2)}) copy-start(f32[2048,768]{1,0:T(8,128)S(1)} %get-tuple-element.151) | copy-start | bytes 18874372
  223.6 19.5 %copy-start.153 = (bf16[768,768]{1,0:T(8,128)(2,1)S(1)}, bf16[768,768]{1,0:T(8,128)(2,1)}, u32[]{:S(2)}) copy-start(bf16[768,768]{1,0:T(8,128)(2,1)} %param.24) | copy-start | bytes 3538948
  247.1 266.4 %all-reduce.76.cloned.1.call-start = ((), (), s32[]{:S(2)}) async-start(), calls=%async_computation.8 | async-start | bytes 6291456 | tf_op jit(solution)/shard_map/psum | solution.py:318
  374.0 7.6 slice-start
  374.0 7.6 slice-start.2
  381.6 5.5 copy-start.3
  393.3 226.1 %reduce-scatter.17.cloned.1.call-start = ((), (), s32[]{:S(2)}) async-start(), calls=%async_computation.11 | async-start | bytes 2654208 | tf_op jit(solution)/shard_map/reduce_scatter | solution.py:348
  401.3 253.6 %reduce-scatter.15.cloned.1.call-start = ((), (), s32[]{:S(2)}) async-start(), calls=%async_computation.9 | async-start | bytes 2654208 | tf_op jit(solution)/shard_map/reduce_scatter | solution.py:347
  413.6 284.0 %reduce-scatter.23.cloned.1.call-start = ((), (), s32[]{:S(2)}) async-start(), calls=%async_computation.16 | async-start | bytes 442368
  513.5 7.6 copy-start.10
  521.1 8.8 copy-start.81
  566.3 7.8 copy-start.8
  566.3 7.8 copy-start.147
  574.1 9.1 copy-start.62
  591.3 5.6 copy-start.85
  591.3 5.6 copy-start.110
  591.3 5.6 copy-start.151
  596.8 5.6 copy-start.95
  596.8 5.6 copy-start.97
  596.8 111.4 %reduce-scatter.25.cloned.1.call-start = ((), (), s32[]{:S(2)}) async-start(), calls=%async_computation.17 | async-start | bytes 442368
  602.4 116.2 %reduce-scatter.21.cloned.1.call-start = ((), (), s32[]{:S(2)}) async-start(), calls=%async_computation.15 | async-start | bytes 884736
  605.3 138.6 %all-gather.9.cloned.1.call-start = ((), (), s32[]{:S(2)}) async-start(), calls=%async_computation.12 | async-start | bytes 1327104 | tf_op jit(solution)/shard_map/all_gather | solution.py:364
  610.5 10.9 %copy-start.83 = (bf16[2,64,3,64]{3,1,2,0:T(8,128)(2,1)S(1)}, bf16[2,64,3,64]{3,1,2,0:T(8,128)(2,1)}, u32[]{:S(2)}) copy-start(bf16[2,64,3,64]{3,1,2,0:T(8,128)(2,1)} %copy-done.82) | copy-start | bytes 147460
  610.5 10.9 %copy-start.111 = (f32[2,3,64]{2,1,0:T(4,128)S(1)}, f32[2,3,64]{2,1,0:T(4,128)}, u32[]{:S(2)}) copy-start(f32[2,3,64]{2,1,0:T(4,128)} %neg.102) | copy-start | bytes 4612
  610.5 10.9 %copy-start.152 = (f32[2,64]{1,0:T(2,128)S(1)}, f32[2,64]{1,0:T(2,128)}, u32[]{:S(2)}) copy-start(f32[2,64]{1,0:T(2,128)} %copy-done.150) | copy-start | bytes 1540
  619.2 5.3 copy-start.133
  619.2 5.3 copy-start.134
  619.2 5.3 copy-start.135
  619.2 5.3 copy-start.136
  619.2 5.3 copy-start.137
  619.2 5.3 copy-start.138
  619.2 5.3 copy-start.139
  619.2 5.3 copy-start.140
  619.2 5.3 copy-start.141
  619.2 5.3 copy-start.142
  621.0 148.7 %all-gather.7.cloned.1.call-start = ((), (), s32[]{:S(2)}) async-start(), calls=%async_computation.10 | async-start | bytes 1327104 | tf_op jit(solution)/shard_map/all_gather | solution.py:361
  656.5 157.0 %reduce-scatter.19.cloned.1.call-start = ((), (), s32[]{:S(2)}) async-start(), calls=%async_computation.14 | async-start | bytes 2211840
  690.4 343.4 %all-gather.11.cloned.1.call-start = ((), (), s32[]{:S(2)}) async-start(), calls=%async_computation.13 | async-start | bytes 15728640 | tf_op jit(solution)/shard_map/all_gather | solution.py:12
  1042.8 6.3 copy-start.1
  (126 other events, 275.5 us)
Sparse Core Ops, SparseCore 0:
  93.2 123.7 all-reduce.71
  247.2 120.0 all-reduce.73
  393.4 120.0 all-reduce.75
  517.3 41.5 reduce-scatter.16
  563.0 42.4 reduce-scatter.14
  609.0 33.7 reduce-scatter.22
  645.9 33.8 reduce-scatter.24
  682.9 34.9 reduce-scatter.20
  719.8 24.0 all-gather.8
  745.6 24.0 all-gather.6
  773.1 40.3 reduce-scatter.18
  815.5 218.1 all-gather.10
